TPU v7x, 128 devices: a whole 4x4x4 slice. The times are simulated.
128 devices in a mesh: req: 32 (over y, z, core), tensor: 4 (over x).
Axes of the slice: x: 4, y: 4, z: 4, core: 2. Of those that a mesh axis runs over, the one named last changes fastest.
Arguments:
- hidden: bfloat16 [32768, 1024], P('req', 'tensor')
- gain: bfloat16 [1024], P('tensor'), may hold values from 0.5 to 1.5
- head: bfloat16 [1024, 32128], P(None, ('req', 'tensor'))
- token_ids: int32 [32768], P('req'), may hold values from 0 to 32127
- lengths: int32 [32], P('req'), may hold values from 1 to 1024, 12288 in all
- prompt_of: int32 [32], P('req'), may hold values from 0 to 3, as said below
Outputs:
- token_logprob: float32 [32768], P(('req', 'tensor'))
- token_entropy: float32 [32768], P(('req', 'tensor'))
- prompt_stats: float32 [4, 2], replicated
Inputs may be any that keep to these rules, and one draw needn't show every extreme that they name: The lengths sum to 12288 and the longest is exactly 1024. `prompt_of`: a prompt may have no responses.
All inputs are finite; a program needn't handle non-finite values. No bound on the sum of `lengths` on one device may be relied on, other than what follows from the above.
Results may differ from a plain program's by a relative error of at most 0.0019.
Values may be sent and summed in bfloat16 or wider, within the bound.
A program may use at most 128 MiB of HBM per device.

v0:
```python
import jax
import jax.numpy as jnp
from jax import lax
from jax.sharding import PartitionSpec as P

PROMPTS = 4
NEG = -1e30
eps = 1e-06


def chunk_stats(normed, piece, vocab_ids, valid, ids):
    logits = lax.dot_general(
        normed, piece, (((1,), (1,)), ((), ())), preferred_element_type=jnp.float32
    )
    logits = jnp.where(valid[None, :], logits, NEG)
    top = jnp.max(logits, axis=1)
    expo = jnp.exp(logits - top[:, None])
    total = jnp.sum(expo, axis=1)
    moment = jnp.sum(expo * logits, axis=1)
    pick = jnp.sum(jnp.where(vocab_ids[None, :] == ids[:, None], logits, 0.0), axis=1)
    return (top, total, moment, pick)


def merge(stats):
    tops = jnp.stack([s[0] for s in stats])
    top = jnp.max(tops, axis=0)
    factor = jnp.exp(tops - top[None, :])
    total = jnp.sum(factor * jnp.stack([s[1] for s in stats]), axis=0)
    moment = jnp.sum(factor * jnp.stack([s[2] for s in stats]), axis=0)
    pick = jnp.sum(jnp.stack([s[3] for s in stats]), axis=0)
    return (top, total, moment, pick)


def local(hidden, gain, head, token_ids, lengths, prompt_of):
    rows, part_width = hidden.shape
    splits = lax.axis_size("tensor")
    column_index = lax.axis_index("tensor")
    req_count = lax.axis_size("req")
    shard_cols = head.shape[1]
    width = part_width * splits
    extra = jnp.zeros((8, part_width), hidden.dtype).at[0].set(gain)
    packed = jnp.concatenate([hidden, extra], axis=0)
    gathered = lax.all_gather(packed, "tensor", axis=1, tiled=True)
    widened = gathered[:rows].astype(jnp.float32)
    gain_full = gathered[rows].astype(jnp.float32)
    scale = lax.rsqrt(jnp.sum(widened * widened, axis=1) / width + eps)
    normed = (widened * scale[:, None] * gain_full[None, :]).astype(jnp.bfloat16)
    head_t = head.T
    chunk = 128
    bounds = [(lo, min(lo + chunk, shard_cols)) for lo in range(0, shard_cols, chunk)]
    stats = []
    for lo, hi in bounds:
        part = head_t[lo:hi]
        if hi - lo < chunk:
            part = jnp.concatenate(
                [part, jnp.zeros((chunk - (hi - lo), part.shape[1]), part.dtype)], axis=0
            )
        piece = lax.all_gather(part, "req", axis=0, tiled=True)
        g = jnp.arange(req_count * chunk, dtype=jnp.int32)
        owner = g // chunk
        offset = lo + g % chunk
        valid = offset < hi
        vocab_ids = jnp.where(valid, (owner * splits + column_index) * shard_cols + offset, -1)
        stats.append(chunk_stats(normed, piece, vocab_ids, valid, token_ids))
    mine = merge(stats)
    everyone = lax.all_gather(jnp.stack(mine), "tensor", axis=0, tiled=False)
    top, total, moment, picked = merge(
        [tuple((everyone[k, j] for j in range(4))) for k in range(splits)]
    )
    positions = jnp.arange(rows, dtype=jnp.int32)
    live = positions < lengths[0]
    safe_total = jnp.where(live, total, 1.0)
    log_norm = top + jnp.log(safe_total)
    logprob = jnp.where(live, picked - log_norm, 0.0)
    entropy = jnp.where(live, log_norm - moment / safe_total, 0.0)
    onehot = (jnp.arange(PROMPTS, dtype=jnp.int32) == prompt_of[0]).astype(jnp.float32)
    summary = jnp.stack([jnp.sum(entropy), jnp.sum(logprob), lengths[0].astype(jnp.float32)])
    summed = lax.psum(onehot[:, None] * summary[None, :], "req")
    prompt_stats = summed[:, :2] / jnp.maximum(summed[:, 2:3], 1.0)
    share = rows // splits
    own_logprob = lax.dynamic_slice_in_dim(logprob, column_index * share, share)
    own_entropy = lax.dynamic_slice_in_dim(entropy, column_index * share, share)
    return (own_logprob, own_entropy, prompt_stats)


def solution(mesh):
    in_specs = (
        P("req", "tensor"),
        P("tensor"),
        P(None, ("req", "tensor")),
        P("req"),
        P("req"),
        P("req"),
    )
    out_specs = (P(("req", "tensor")), P(("req", "tensor")), P())
    return jax.shard_map(local, mesh=mesh, in_specs=in_specs, out_specs=out_specs, check_vma=False)
```

profile of v0, /device:TPU:1, one launch (start us, length us, event | category | flops | bytes accessed | tf_op | source)
XLA Modules:
  0.0 288.1 jit_solution(5569118323441243432)
XLA Ops:
  7.2 0.0 all-gather.6.cloned.1.call-start
  7.2 0.7 reshape.148
  7.9 1.9 fusion.6
  9.8 0.0 all-gather.6.cloned.1.call-update
  9.8 0.0 all-gather.8.cloned.1.call-start
  9.8 1.7 slice.104
  11.5 0.0 all-gather.8.cloned.1.call-update
  11.5 0.0 all-gather.10.cloned.1.call-start
  11.6 1.0 slice.105
  12.6 0.8 concatenate.9
  13.3 0.0 all-gather.10.cloned.1.call-update
  14.7 31.1 %all-gather.6.cloned.1.call-done = bf16[1032,1024]{1,0:T(8,128)(2,1)} async-done(((bf16[1032,256]{1,0:T(8,128)(2,1)}), bf16[1032,1024]{1,0:T(8,128)(2,1)}) %all-gather.6.cloned.1.call-update) | async-done | bytes 2113552 | tf_op jit(solution)/shard_map/all_gather | solution.py:43
  45.8 2.1 fusion.2
  47.9 0.7 slice_convert_fusion
  48.6 61.1 %all-gather.8.cloned.1.call-done = bf16[4096,1024]{0,1:T(8,128)(2,1)} async-done(((bf16[128,1024]{0,1:T(8,128)(2,1)}), bf16[4096,1024]{0,1:T(8,128)(2,1)}) %all-gather.8.cloned.1.call-update) | async-done | bytes 8388624 | tf_op jit(solution)/shard_map/all_gather | solution.py:58
  109.7 16.5 %select_reduce_fusion.3 = (f32[1024]{0:T(1024)S(1)}, f32[1024,4096]{1,0:T(8,128)}) fusion(pred[4096]{0:T(1024)(128)(4,1)S(1)} %get-tuple-element.53, bf16[4096,1024]{0,1:T(8,128)(2,1)} %all-gather.8.cloned.1.call-done, f32[1024]{0:T(1024)S(1)} %bitcast.69, f32[1024]{0:T(1024)S(1)} %add_rsqrt_fusion, bf16[1032,1024]{1,0:T(8,128)(2,1)} %all-gather.6.cloned.1.call-done), kind=kOutput, calls=%fused_computation.9 | convolution fusion | flops 8602516480 | bytes 27279360 | tf_op jit(solution)/shard_map/dot_general | solution.py:12
  126.2 44.3 %all-gather.10.cloned.1.call-done = bf16[4096,1024]{0,1:T(8,128)(2,1)} async-done(((bf16[128,1024]{0,1:T(8,128)(2,1)}), bf16[4096,1024]{0,1:T(8,128)(2,1)}) %all-gather.10.cloned.1.call-update) | async-done | bytes 8388624 | tf_op jit(solution)/shard_map/all_gather | solution.py:58
  170.5 0.0 slice-start.3
  170.5 0.0 copy-start.1
  170.5 14.7 %select_reduce_fusion.2 = (f32[1024]{0:T(1024)S(1)}, f32[1024,4096]{1,0:T(8,128)}) fusion(pred[4096]{0:T(1024)(128)(4,1)S(1)} %get-tuple-element.54, bf16[4096,1024]{0,1:T(8,128)(2,1)} %all-gather.10.cloned.1.call-done, f32[1024]{0:T(1024)S(1)} %bitcast.70, f32[1024]{0:T(1024)S(1)} %add_rsqrt_fusion, bf16[1032,1024]{1,0:T(8,128)(2,1)S(1)} %copy-done), kind=kOutput, calls=%fused_computation.8 | convolution fusion | flops 8602516480 | bytes 27279360 | tf_op jit(solution)/shard_map/dot_general | solution.py:12
  185.2 0.0 slice-done.1
  185.3 0.0 slice-done.2
  185.3 17.7 %fusion = (f32[1024]{0:T(1024)S(1)}, f32[1024]{0:T(1024)S(1)}, f32[1024]{0:T(1024)S(1)}, f32[1024]{0:T(1024)S(1)}, f32[1024]{0:T(1024)S(1)}, /*index=5*/f32[1024]{0:T(1024)S(1)}) fusion(f32[1024,4096]{1,0:T(8,128)} %get-tuple-element.48, f32[1024]{0:T(1024)S(1)} %get-tuple-element.47, pred[4096]{0:T(1024)(128)(4,1)S(1)} %get-tuple-element.54, ...), kind=kLoop, calls=%fused_computation.5 | loop fusion | flops 67102720 | bytes 33632256 | tf_op jit(solution)/shard_map/reduce_sum | solution.py:18
  203.1 9.6 %all-gather.1 = f32[4,4,1024]{2,1,0:T(4,128)S(1)} all-gather(f32[1,4,1024]{2,1,0:T(4,128)S(1)} %maximum_bitcast_fusion), channel_id=2, replica_groups=mesh['req'=32,'tensor'=4] {'tensor'}, dimensions={0}, use_global_device_ids=true | all-gather | bytes 81920 | tf_op jit(solution)/shard_map/all_gather | solution.py:66
  212.7 0.1 fusion.21
  212.8 0.6 fusion.33
  213.4 1.4 pad_maximum_fusion
  214.8 0.1 broadcast_multiply_fusion
  214.9 64.9 %psum.7 = f32[4,3]{0,1:T(4,128)S(1)} all-reduce(f32[4,3]{0,1:T(4,128)S(1)} %broadcast_multiply_fusion), channel_id=1, replica_groups=mesh['req'=32,'tensor'=4] {'req'}, use_global_device_ids=true, to_apply=%region_15.16 | all-reduce | flops 12 | bytes 96 | tf_op jit(solution)/shard_map/psum | solution.py:78
  279.7 0.6 slice_divide_fusion
  280.3 0.6 dynamic_slice.7
  281.0 0.6 dynamic_slice.6
  (21 shorter events, 0.2 us)
Async XLA Ops:
  7.2 38.7 %all-gather.6.cloned.1.call-start = ((), (), s32[]{:S(2)}) async-start(), calls=%async_computation | async-start | bytes 2641920 | tf_op jit(solution)/shard_map/all_gather | solution.py:43
  9.8 99.9 %all-gather.8.cloned.1.call-start = ((), (), s32[]{:S(2)}) async-start(), calls=%async_computation.1 | async-start | bytes 8650752 | tf_op jit(solution)/shard_map/all_gather | solution.py:58
  11.5 158.9 %all-gather.10.cloned.1.call-start = ((), (), s32[]{:S(2)}) async-start(), calls=%async_computation.2 | async-start | bytes 8650752 | tf_op jit(solution)/shard_map/all_gather | solution.py:58
  109.7 60.8 %copy-start = (bf16[1032,1024]{1,0:T(8,128)(2,1)S(1)}, bf16[1032,1024]{1,0:T(8,128)(2,1)}, u32[]{:S(2)}) copy-start(bf16[1032,1024]{1,0:T(8,128)(2,1)} %all-gather.6.cloned.1.call-done) | copy-start | bytes 6340612
  170.5 14.8 %slice-start = ((s8[16777216]{0:T(1024)(128)(4,1)}), s8[4194304]{0:T(1024)(128)(4,1)S(1)}, s32[]{:S(2)}) async-start(s8[16777216]{0:T(1024)(128)(4,1)} %bitcast.51), calls=%async_computation.3 | async-start | bytes 8388608
  170.5 14.8 %slice-start.1 = ((s8[16777216]{0:T(1024)(128)(4,1)}), s8[4194304]{0:T(1024)(128)(4,1)S(1)}, s32[]{:S(2)}) async-start(s8[16777216]{0:T(1024)(128)(4,1)} %bitcast.51), calls=%async_computation.4 | async-start | bytes 8388608
  170.5 14.8 %slice-start.2 = ((s8[16777216]{0:T(1024)(128)(4,1)}), s8[4194304]{0:T(1024)(128)(4,1)S(1)}, s32[]{:S(2)}) async-start(s8[16777216]{0:T(1024)(128)(4,1)} %bitcast.51), calls=%async_computation.5 | async-start | bytes 8388608
  170.5 14.8 %slice-start.3 = ((s8[16777216]{0:T(1024)(128)(4,1)}), s8[4194304]{0:T(1024)(128)(4,1)S(1)}, s32[]{:S(2)}) async-start(s8[16777216]{0:T(1024)(128)(4,1)} %bitcast.51), calls=%async_computation.6 | async-start | bytes 8388608
  170.5 14.8 %copy-start.1 = (s32[1024]{0:T(1024)S(1)}, s32[1024]{0:T(1024)}, u32[]{:S(2)}) copy-start(s32[1024]{0:T(1024)} %param.11) | copy-start | bytes 12292
Sparse Core Ops, SparseCore 0:
  9.9 35.8 all-gather.5
  48.0 61.6 all-gather.7
  111.9 58.5 all-gather.9
where the time goes:
time: 288 us
  waiting for transfers between devices  137 us (48%)
  blocking collectives  74.4 us (26%)
  matrix products  31.2 us (11%)
  other arithmetic  25.2 us (9%)
  between operations  15.2 us (5%)
  local copies, waits for them, and re-layouts  5.38 us (2%)
    all_gather x2, waiting for transfers between devices, local(): piece = lax.all_gather(part, 'req', axis=0, tiled=True)  105 us
    psum x1, blocking collectives, local(): summed = lax.psum(onehot[:, None] * summary[None, :], 'req')  64.9 us
    dot_general x2, matrix products, chunk_stats(): lax.dot_general(normed, piece, (((1,), (1,)), ((), ())), preferred_elemen...  31.2 us
    all_gather x1, waiting for transfers between devices, local(): gathered = lax.all_gather(packed, 'tensor', axis=1, tiled=True)  31.1 us
    reduce_sum x1, other arithmetic, chunk_stats(): total = jnp.sum(expo, axis=1)  17.7 us
    all_gather x1, blocking collectives, local(): everyone = lax.all_gather(jnp.stack(mine), 'tensor', axis=0, tiled=False)  9.59 us
  transfers between devices with their start and end apart: 3, of which 3 were waited for; matrix products, arithmetic and copies ran while one was open for 8% of the time, Pallas kernels for 0%

commit v1 on v0

--- a/solution.py
+++ b/solution.py
@@ -40,7 +40,28 @@
     width = part_width * splits
     extra = jnp.zeros((8, part_width), hidden.dtype).at[0].set(gain)
     packed = jnp.concatenate([hidden, extra], axis=0)
-    gathered = lax.all_gather(packed, "tensor", axis=1, tiled=True)
+    s_next = lax.axis_size("tensor")
+    local_out, low, a_next = (s_next, lax.axis_index("tensor"), packed.shape[1])
+    leaves = []
+    for rr in [*range(local_out)]:
+        leaves.append((rr, (rr + 1) % local_out))
+    made = []
+    for rr in [*range(local_out)]:
+        made.append((rr, (rr - 1) % local_out))
+    gathered = jnp.zeros((*packed.shape[:1], local_out * a_next, *packed.shape[2:]), packed.dtype)
+    gathered = lax.dynamic_update_slice_in_dim(gathered, packed, low * a_next, axis=1)
+    ready = block_out = packed
+    part_next = local_out // 2
+    for p in [*range(1, part_next + 1)]:
+        ready = lax.ppermute(ready, perm=leaves, axis_name="tensor")
+        gathered = lax.dynamic_update_slice_in_dim(
+            gathered, ready, (low - p) % local_out * a_next, axis=1
+        )
+        if p < local_out - part_next:
+            block_out = lax.ppermute(block_out, axis_name="tensor", perm=made)
+            gathered = lax.dynamic_update_slice_in_dim(
+                gathered, block_out, (low + p) % local_out * a_next, axis=1
+            )
     widened = gathered[:rows].astype(jnp.float32)
     gain_full = gathered[rows].astype(jnp.float32)
     scale = lax.rsqrt(jnp.sum(widened * widened, axis=1) / width + eps)

time: 288 us -> 252 us (0.88)
  waiting for transfers between devices: 137 us -> 99.1 us
  starting transfers between devices: 0.12 us -> 3.91 us
  other arithmetic: 25.2 us -> 21.5 us
    all_gather x1 -> x0, waiting for transfers between devices: 31.1 us -> none  [local(): gathered = lax.all_gather(packed, 'tensor', axis=1, tiled=True)]
    all_gather x2, waiting for transfers between devices: 105 us -> 77.5 us  [local(): piece = lax.all_gather(part, 'req', axis=0, tiled=True)]
    ppermute x0 -> x3, waiting for transfers between devices: none -> 21.6 us  [the longest x2 21.6 us: local(): ready = lax.ppermute(ready, perm=leaves, axis_name='tensor')]
    ppermute x0 -> x3, starting transfers between devices: none -> 3.83 us  [the longest x2 2.48 us: local(): ready = lax.ppermute(ready, perm=leaves, axis_name='tensor')]
  transfers between devices with their start and end apart: 3 -> 5, of which waited for: 3 -> 4; matrix products, arithmetic and copies ran while one was open for 8% -> 8% of each run, Pallas kernels for 0% -> 0%
where the time goes in v1:
time: 252 us
  waiting for transfers between devices  99.1 us (39%)
  blocking collectives  74.4 us (30%)
  matrix products  29.3 us (12%)
  other arithmetic  21.5 us (9%)
  between operations  15.6 us (6%)
  local copies, waits for them, and re-layouts  7.93 us (3%)
  starting transfers between devices  3.91 us (2%)
    all_gather x2, waiting for transfers between devices, local(): piece = lax.all_gather(part, 'req', axis=0, tiled=True)  77.5 us
    psum x1, blocking collectives, local(): summed = lax.psum(onehot[:, None] * summary[None, :], 'req')  64.8 us
    dot_general x2, matrix products, chunk_stats(): lax.dot_general(normed, piece, (((1,), (1,)), ((), ())), preferred_elemen...  29.3 us
    ppermute x2, waiting for transfers between devices, local(): ready = lax.ppermute(ready, perm=leaves, axis_name='tensor')  21.6 us
    reduce_sum x1, other arithmetic, chunk_stats(): total = jnp.sum(expo, axis=1)  18 us
    all_gather x1, blocking collectives, local(): everyone = lax.all_gather(jnp.stack(mine), 'tensor', axis=0, tiled=False)  9.62 us
  transfers between devices with their start and end apart: 5, of which 4 were waited for; matrix products, arithmetic and copies ran while one was open for 8% of the time, Pallas kernels for 0%

profile of v1, /device:TPU:1, one launch (start us, length us, event | category | flops | bytes accessed | tf_op | source)
XLA Modules:
  0.0 251.8 jit_solution(1732280276588180706)
XLA Ops:
  7.2 0.0 all-gather.5.cloned.1.call-start
  7.2 1.7 slice.104
  8.9 0.0 all-gather.5.cloned.1.call-update
  9.0 0.0 all-gather.7.cloned.1.call-start
  9.0 1.0 slice.105
  10.0 0.8 concatenate.9
  10.8 0.7 reshape.148
  11.4 0.3 broadcast_in_dim.54
  11.7 0.1 fusion.6
  11.8 2.1 collective-permute-start
  13.9 1.3 collective-permute-start.1
  15.9 10.6 %collective-permute-done = bf16[1032,256]{1,0:T(8,128)(2,1)S(1)} collective-permute-done((bf16[1032,256]{1,0:T(8,128)(2,1)S(1)}, bf16[1032,256]{1,0:T(8,128)(2,1)S(1)}, u32[]{:S(2)}, u32[]{:S(2)}) %collective-permute-start) | collective-permute-done | bytes 528416 | tf_op jit(solution)/shard_map/ppermute | solution.py:56
  26.5 0.4 collective-permute-start.2
  27.6 0.1 constant_dynamic-update-slice_fusion.2
  27.7 1.1 constant_dynamic-update-slice_fusion.1
  28.8 11.0 %collective-permute-done.2 = bf16[1032,256]{1,0:T(8,128)(2,1)} collective-permute-done((bf16[1032,256]{1,0:T(8,128)(2,1)S(1)}, bf16[1032,256]{1,0:T(8,128)(2,1)}, u32[]{:S(2)}, u32[]{:S(2)}) %collective-permute-start.2) | collective-permute-done | bytes 528416 | tf_op jit(solution)/shard_map/ppermute | solution.py:56
  39.8 1.1 constant_dynamic-update-slice_fusion
  40.9 0.5 fusion.2
  41.4 31.3 %all-gather.5.cloned.1.call-done = bf16[4096,1024]{0,1:T(8,128)(2,1)} async-done(((bf16[128,1024]{0,1:T(8,128)(2,1)}), bf16[4096,1024]{0,1:T(8,128)(2,1)}) %all-gather.5.cloned.1.call-update) | async-done | bytes 8388624 | tf_op jit(solution)/shard_map/all_gather | solution.py:79
  72.8 14.6 %select_reduce_fusion.3 = (f32[1024]{0:T(1024)S(1)}, f32[1024,4096]{1,0:T(8,128)}) fusion(pred[4096]{0:T(1024)(128)(4,1)S(1)} %get-tuple-element.55, bf16[4096,1024]{0,1:T(8,128)(2,1)} %all-gather.5.cloned.1.call-done, f32[1024]{0:T(1024)S(1)} %bitcast.69, f32[1024]{0:T(1024)S(1)} %add_rsqrt_fusion, bf16[1032,1024]{1,0:T(8,128)(2,1)S(1)} %constant_dynamic-update-slice_fusion), kind=kOutput, calls=%fused_computation.9 | convolution fusion | flops 8602516480 | bytes 27279360 | tf_op jit(solution)/shard_map/dot_general | solution.py:12
  87.3 46.2 %all-gather.7.cloned.1.call-done = bf16[4096,1024]{0,1:T(8,128)(2,1)} async-done(((bf16[128,1024]{0,1:T(8,128)(2,1)}), bf16[4096,1024]{0,1:T(8,128)(2,1)}) %all-gather.7.cloned.1.call-update) | async-done | bytes 8388624 | tf_op jit(solution)/shard_map/all_gather | solution.py:79
  133.5 14.7 %select_reduce_fusion.2 = (f32[1024]{0:T(1024)S(1)}, f32[1024,4096]{1,0:T(8,128)}) fusion(pred[4096]{0:T(1024)(128)(4,1)S(1)} %get-tuple-element.56, bf16[4096,1024]{0,1:T(8,128)(2,1)} %all-gather.7.cloned.1.call-done, f32[1024]{0:T(1024)S(1)} %bitcast.70, f32[1024]{0:T(1024)S(1)} %add_rsqrt_fusion, bf16[1032,1024]{1,0:T(8,128)(2,1)S(1)} %constant_dynamic-update-slice_fusion), kind=kOutput, calls=%fused_computation.8 | convolution fusion | flops 8602516480 | bytes 27279360 | tf_op jit(solution)/shard_map/dot_general | solution.py:12
  148.3 18.0 %fusion = (f32[1024]{0:T(1024)S(1)}, f32[1024]{0:T(1024)S(1)}, f32[1024]{0:T(1024)S(1)}, f32[1024]{0:T(1024)S(1)}, f32[1024]{0:T(1024)S(1)}, /*index=5*/f32[1024]{0:T(1024)S(1)}) fusion(f32[1024,4096]{1,0:T(8,128)} %get-tuple-element.50, f32[1024]{0:T(1024)S(1)} %get-tuple-element.49, pred[4096]{0:T(1024)(128)(4,1)S(1)} %get-tuple-element.56, ...), kind=kLoop, calls=%fused_computation.5 | loop fusion | flops 67102720 | bytes 33632256 | tf_op jit(solution)/shard_map/reduce_sum | solution.py:18
  166.4 9.6 %all-gather.1 = f32[4,4,1024]{2,1,0:T(4,128)S(1)} all-gather(f32[1,4,1024]{2,1,0:T(4,128)S(1)} %maximum_bitcast_fusion), channel_id=2, replica_groups=mesh['req'=32,'tensor'=4] {'tensor'}, dimensions={0}, use_global_device_ids=true | all-gather | bytes 81920 | tf_op jit(solution)/shard_map/all_gather | solution.py:87
  176.1 0.1 fusion.21
  176.2 0.6 fusion.33
  176.8 1.4 pad_maximum_fusion
  178.2 0.1 broadcast_multiply_fusion
  178.2 64.8 %psum.7 = f32[4,3]{0,1:T(4,128)S(1)} all-reduce(f32[4,3]{0,1:T(4,128)S(1)} %broadcast_multiply_fusion), channel_id=1, replica_groups=mesh['req'=32,'tensor'=4] {'req'}, use_global_device_ids=true, to_apply=%region_15.16 | all-reduce | flops 12 | bytes 96 | tf_op jit(solution)/shard_map/psum | solution.py:99
  243.1 0.6 slice_divide_fusion
  243.6 0.6 dynamic_slice.7
  244.3 0.6 dynamic_slice.6
  (28 shorter events, 0.2 us)
Async XLA Ops:
  7.2 4.5 %copy-start = (bf16[1024,256]{1,0:T(8,128)(2,1)S(1)}, bf16[1024,256]{1,0:T(8,128)(2,1)}, u32[]{:S(2)}) copy-start(bf16[1024,256]{1,0:T(8,128)(2,1)} %param.8) | copy-start | bytes 1572868
  7.2 65.6 %all-gather.5.cloned.1.call-start = ((), (), s32[]{:S(2)}) async-start(), calls=%async_computation | async-start | bytes 8650752 | tf_op jit(solution)/shard_map/all_gather | solution.py:79
  9.0 124.5 %all-gather.7.cloned.1.call-start = ((), (), s32[]{:S(2)}) async-start(), calls=%async_computation.1 | async-start | bytes 8650752 | tf_op jit(solution)/shard_map/all_gather | solution.py:79
  11.8 14.7 %collective-permute-start = (bf16[1032,256]{1,0:T(8,128)(2,1)S(1)}, bf16[1032,256]{1,0:T(8,128)(2,1)S(1)}, u32[]{:S(2)}, u32[]{:S(2)}) collective-permute-start(bf16[1032,256]{1,0:T(8,128)(2,1)S(1)} %get-tuple-element.29), channel_id=1, source_target_pairs={{0,1},{1,2},{2,3},{3,0},{4,5},{5,6},{6,7},{7,4},{8,9},{9,10},{10,1... | collective-permute-start | bytes 1585160 | tf_op jit(solution)/shard_map/ppermute | solution.py:56
  13.9 13.7 %collective-permute-start.1 = (bf16[1032,256]{1,0:T(8,128)(2,1)S(1)}, bf16[1032,256]{1,0:T(8,128)(2,1)}, u32[]{:S(2)}, u32[]{:S(2)}) collective-permute-start(bf16[1032,256]{1,0:T(8,128)(2,1)S(1)} %get-tuple-element.29), channel_id=1, source_target_pairs={{0,3},{1,0},{2,1},{3,2},{4,7},{5,4},{6,5},{7,6},{8,11},{9,8},{10,9... | collective-permute-start | bytes 1585160 | tf_op jit(solution)/shard_map/ppermute | solution.py:61
  26.5 13.3 %collective-permute-start.2 = (bf16[1032,256]{1,0:T(8,128)(2,1)S(1)}, bf16[1032,256]{1,0:T(8,128)(2,1)}, u32[]{:S(2)}, u32[]{:S(2)}) collective-permute-start(bf16[1032,256]{1,0:T(8,128)(2,1)S(1)} %collective-permute-done), channel_id=1, source_target_pairs={{0,1},{1,2},{2,3},{3,0},{4,5},{5,6},{6,7},{7,4},{8,9},{9,10},{10,1... | collective-permute-start | bytes 1585160 | tf_op jit(solution)/shard_map/ppermute | solution.py:56
  133.5 14.8 %slice-start = ((s8[16777216]{0:T(1024)(128)(4,1)}), s8[4194304]{0:T(1024)(128)(4,1)S(1)}, s32[]{:S(2)}) async-start(s8[16777216]{0:T(1024)(128)(4,1)} %bitcast.51), calls=%async_computation.2 | async-start | bytes 8388608
  133.5 14.8 %slice-start.1 = ((s8[16777216]{0:T(1024)(128)(4,1)}), s8[4194304]{0:T(1024)(128)(4,1)S(1)}, s32[]{:S(2)}) async-start(s8[16777216]{0:T(1024)(128)(4,1)} %bitcast.51), calls=%async_computation.3 | async-start | bytes 8388608
  133.5 14.8 %slice-start.2 = ((s8[16777216]{0:T(1024)(128)(4,1)}), s8[4194304]{0:T(1024)(128)(4,1)S(1)}, s32[]{:S(2)}) async-start(s8[16777216]{0:T(1024)(128)(4,1)} %bitcast.51), calls=%async_computation.4 | async-start | bytes 8388608
  133.5 14.8 %slice-start.3 = ((s8[16777216]{0:T(1024)(128)(4,1)}), s8[4194304]{0:T(1024)(128)(4,1)S(1)}, s32[]{:S(2)}) async-start(s8[16777216]{0:T(1024)(128)(4,1)} %bitcast.51), calls=%async_computation.5 | async-start | bytes 8388608
  133.5 14.8 %copy-start.1 = (s32[1024]{0:T(1024)S(1)}, s32[1024]{0:T(1024)}, u32[]{:S(2)}) copy-start(s32[1024]{0:T(1024)} %param.11) | copy-start | bytes 12292
Sparse Core Ops, SparseCore 0:
  10.2 62.5 all-gather.4
  74.9 58.5 all-gather.6
